TPU v7x, 512 devices: a whole 4x4x16 slice. The times are simulated.
512 devices in a mesh: grp: 16 (over y, x), tok: 32 (over z, core).
Axes of the slice: x: 4, y: 4, z: 16, core: 2. Of those that a mesh axis runs over, the one named last changes fastest.
Arguments:
- hidden_in: bfloat16 [16, 4096, 1024], P('grp', 'tok'), may hold values from -6 to 6
- lengths: int32 [16, 3], P('grp'), may hold values from 1 to 3072, 4096 in all within a row
- prefix_cache: bfloat16 [16, 512, 512], P('grp', 'tok'), may hold values from -2600 to 2600
- routes: int32 [16, 4096, 8], P('grp', 'tok'), may hold values from 0 to 31, all different within a row; in each aligned block of 128 rows (0 to 127, 128 to 255, ..., all dimensions but the last counted through in order) at most 40 rows name the same one
- gates: float32 [16, 4096, 8], P('grp', 'tok'), may hold values from 0.05 to 0.4
- attn_gain: float32 [1024], replicated, may hold values from 0.1 to 1.9
- w_qkv: bfloat16 [1024, 1024], P('grp', 'tok'), may hold values from -0.75 to 0.75
- w_out: bfloat16 [512, 1024], P('grp', 'tok'), may hold values from -0.25 to 0.25
- moe_gain: float32 [1024], replicated, may hold values from 0.1 to 1.9
- expert_gate_up: bfloat16 [32, 1024, 1024], P('tok', 'grp'), may hold values from -0.1875 to 0.1875
- expert_down: bfloat16 [32, 512, 1024], P('tok', 'grp'), may hold values from -0.25 to 0.25
Outputs:
- hidden_out: bfloat16 [16, 4096, 1024], P('grp', 'tok')
- suffix_cache: bfloat16 [16, 4096, 512], P('grp', 'tok')
Inputs may be any that keep to these rules, and one draw needn't show every extreme that they name: Each group's 3 lengths sum to 4096; no request is longer than 3072 tokens, and some request of every draw has exactly 3072. `routes`: each token names 8 different experts. Among the 128 tokens of one device no expert is named more than 40 times, a bound that some block reaches.
All inputs are finite; a program needn't handle non-finite values.
Results may differ from a plain program's by a relative error of at most 0.02.
Values may be sent and summed in bfloat16 or wider, within the bound.
A program may use at most 128 MiB of HBM per device.

v0:
```python
import jax
import jax.numpy as jnp
from jax import lax
from jax.sharding import PartitionSpec as P

HEADS = 8
KV_HEADS = 4
HEAD_DIM = 64
FF = 512
EXPERTS = 32
TOP = 8
CAP = 40
epsilon = 1e-05
score_scale = 0.015625
rope_base = 10000.0
big_negative = -1e30


def rms_scale(values, gain):
    values = values.astype(jnp.float32)
    mean_square = jnp.mean(values * values, axis=-1, keepdims=True)
    return values * lax.rsqrt(mean_square + epsilon) * gain


def request_layout(group_lengths, token_index):
    ends = jnp.cumsum(group_lengths)
    starts = ends - group_lengths
    segment = jnp.sum((token_index[:, None] >= ends[None, :]).astype(jnp.int32), axis=1)
    match = segment[:, None] == jnp.arange(group_lengths.shape[0], dtype=jnp.int32)[None, :]
    offset = token_index - jnp.sum(jnp.where(match, starts[None, :], 0), axis=1)
    return (segment, offset)


def rotate(values, position):
    half_width = values.shape[-1] // 2
    frequency = rope_base ** (-jnp.arange(half_width, dtype=jnp.float32) * 2.0 / values.shape[-1])
    angle = position.astype(jnp.float32)[:, None] * frequency[None, :]
    cosine = jnp.cos(angle)[:, None, :]
    sine = jnp.sin(angle)[:, None, :]
    first = values[..., :half_width]
    second = values[..., half_width:]
    return jnp.concatenate(
        [first * cosine - second * sine, second * cosine + first * sine], axis=-1
    )


def attend(carry, grouped, keys_values, allowed):
    best, total, mixed = carry
    key_count = keys_values.shape[0]
    key_width = KV_HEADS * HEAD_DIM
    key_heads = keys_values[:, :key_width].reshape(key_count, KV_HEADS, HEAD_DIM).transpose(1, 0, 2)
    value_heads = (
        keys_values[:, key_width:].reshape(key_count, KV_HEADS, HEAD_DIM).transpose(1, 0, 2)
    )
    scores = (
        jnp.einsum("kqd,knd->kqn", grouped, key_heads, preferred_element_type=jnp.float32)
        * score_scale
    )
    if allowed is not None:
        row_count = grouped.shape[1]
        share = row_count // allowed.shape[0]
        mask = jnp.broadcast_to(allowed[:, None, :], (allowed.shape[0], share, key_count)).reshape(
            row_count, key_count
        )
        scores = jnp.where(mask[None], scores, big_negative)
    new_best = jnp.maximum(best, jnp.max(scores, axis=-1))
    factor = jnp.exp(best - new_best)
    probs = jnp.exp(scores - new_best[..., None])
    total = total * factor + jnp.sum(probs, axis=-1)
    mixed = mixed * factor[..., None] + jnp.einsum(
        "kqn,knd->kqd", probs.astype(jnp.bfloat16), value_heads, preferred_element_type=jnp.float32
    )
    return (new_best, total, mixed)


def local(
    hidden_in,
    lengths,
    prefix_cache,
    routes,
    gates,
    attn_gain,
    w_qkv,
    w_out,
    moe_gain,
    expert_gate_up,
    expert_down,
):
    tokens_here = hidden_in[0]
    tok_count = tokens_here.shape[0]
    axis_count = lax.axis_size("tok")
    device_place = lax.axis_index("tok")
    group_lengths = lengths[0]
    token_index = device_place * tok_count + jnp.arange(tok_count, dtype=jnp.int32)
    segment, offset = request_layout(group_lengths, token_index)
    position = prefix_cache.shape[1] * axis_count + offset
    query_width = HEADS * HEAD_DIM
    key_width = KV_HEADS * HEAD_DIM
    group_share = HEADS // KV_HEADS
    normed = rms_scale(tokens_here, attn_gain).astype(jnp.bfloat16)
    columns = lax.all_gather(w_qkv, "tok", axis=1, tiled=True)
    sliced = normed
    projected = jnp.dot(
        sliced,
        lax.all_gather(columns, "grp", axis=0, tiled=True),
        preferred_element_type=jnp.float32,
    )
    query = rotate(projected[:, :query_width].reshape(tok_count, HEADS, HEAD_DIM), position).astype(
        jnp.bfloat16
    )
    keys_new = rotate(
        projected[:, query_width : query_width + key_width].reshape(tok_count, KV_HEADS, HEAD_DIM),
        position,
    ).astype(jnp.bfloat16)
    values_new = projected[:, query_width + key_width :].astype(jnp.bfloat16)
    suffix_cache = jnp.concatenate([keys_new.reshape(tok_count, key_width), values_new], axis=1)
    row_count = tok_count * group_share
    grouped = (
        query.reshape(tok_count, KV_HEADS, group_share, HEAD_DIM)
        .transpose(1, 0, 2, 3)
        .reshape(KV_HEADS, row_count, HEAD_DIM)
    )
    start_carry = (
        jnp.full((KV_HEADS, row_count), big_negative, jnp.float32),
        jnp.zeros((KV_HEADS, row_count), jnp.float32),
        jnp.zeros((KV_HEADS, row_count, HEAD_DIM), jnp.float32),
    )
    carry = attend(
        start_carry, grouped, lax.all_gather(prefix_cache[0], "tok", axis=0, tiled=True), None
    )
    piece = lax.all_gather(suffix_cache, "tok", axis=0, tiled=True)
    key_index = jnp.arange(piece.shape[0], dtype=jnp.int32)
    key_segment, key_offset = request_layout(group_lengths, key_index)
    earlier = key_index[None, :] <= token_index[:, None]
    same_request = key_segment[None, :] == segment[:, None]
    carry = attend(carry, grouped, piece, earlier & same_request & (key_index[None, :] >= 0))
    best, total, mixed = carry
    attended = (mixed / total[..., None]).reshape(KV_HEADS, tok_count, group_share, HEAD_DIM)
    attended = attended.transpose(1, 0, 2, 3).reshape(tok_count, query_width).astype(jnp.bfloat16)
    out_columns = lax.all_gather(w_out, "tok", axis=1, tiled=True)
    sliced = attended
    projected_out = jnp.dot(
        sliced,
        lax.all_gather(out_columns, "grp", axis=0, tiled=True),
        preferred_element_type=jnp.float32,
    )
    after_attention = tokens_here.astype(jnp.float32) + projected_out
    moe_in = rms_scale(after_attention, moe_gain).astype(jnp.bfloat16)
    model_width = moe_in.shape[1]
    flat_routes = routes[0].reshape(-1)
    onehot = (flat_routes[:, None] == jnp.arange(EXPERTS, dtype=jnp.int32)[None, :]).astype(
        jnp.int32
    )
    slot_rank = jnp.sum(jnp.cumsum(onehot, axis=0) * onehot, axis=1) - 1
    slot_index = flat_routes * CAP + slot_rank
    source_token = jnp.arange(flat_routes.shape[0], dtype=jnp.int32) // TOP
    outgoing = (
        jnp.zeros((EXPERTS * CAP, model_width), jnp.bfloat16)
        .at[slot_index]
        .set(moe_in[source_token])
    )
    arrived = lax.all_to_all(
        outgoing.reshape(EXPERTS, CAP, model_width), "tok", split_axis=0, concat_axis=1, tiled=True
    )
    sliced = arrived
    hidden_pair = jnp.einsum(
        "erd,edf->erf",
        sliced,
        lax.all_gather(expert_gate_up, "grp", axis=1, tiled=True),
        preferred_element_type=jnp.float32,
    )
    activated = (jax.nn.silu(hidden_pair[..., :FF]) * hidden_pair[..., FF:]).astype(jnp.bfloat16)
    sliced = activated
    expert_result = jnp.einsum(
        "erf,efd->erd",
        sliced,
        lax.all_gather(expert_down, "grp", axis=1, tiled=True),
        preferred_element_type=jnp.float32,
    ).astype(jnp.bfloat16)
    returned = lax.all_to_all(
        expert_result, "tok", split_axis=1, concat_axis=0, tiled=True
    ).reshape(EXPERTS * CAP, -1)
    weighted = returned[slot_index].astype(jnp.float32) * gates[0].reshape(-1)[:, None]
    moe_out = jnp.sum(weighted.reshape(tok_count, TOP, -1), axis=1)
    hidden_out = (after_attention + moe_out).astype(jnp.bfloat16)
    return (hidden_out[None], suffix_cache[None])


def solution(mesh):
    return jax.shard_map(
        local,
        mesh=mesh,
        in_specs=(
            P("grp", "tok", None),
            P("grp", None),
            P("grp", "tok", None),
            P("grp", "tok", None),
            P("grp", "tok", None),
            P(),
            P("grp", "tok"),
            P("grp", "tok"),
            P(),
            P("tok", "grp", None),
            P("tok", "grp", None),
        ),
        out_specs=(P("grp", "tok", None), P("grp", "tok", None)),
        check_vma=False,
    )
```

profile of v0, /device:TPU:32, one launch (start us, length us, event | category | flops | bytes accessed | tf_op | source)
XLA Modules:
  0.0 593.4 jit_solution(6562197188762396571)
XLA Ops:
  7.2 35.0 %all_gather.24 = bf16[64,1024]{0,1:T(8,128)(2,1)S(1)} all-gather(bf16[64,32]{0,1:T(8,128)(2,1)} %param.17), channel_id=1, replica_groups=mesh['grp'=16,'tok'=32] {'tok'}, dimensions={1}, use_global_device_ids=true | all-gather | bytes 135168 | tf_op jit(solution)/shard_map/all_gather | solution.py:101
  42.3 0.8 copy.106
  43.1 0.8 reduce-window.10
  44.1 0.7 fusion.38
  44.8 1.1 fusion.26
  46.1 55.2 %all-gather.7.cloned.1.call-done = bf16[1024,1024]{1,0:T(8,128)(2,1)} async-done(((bf16[64,1024]{1,0:T(8,128)(2,1)}), bf16[1024,1024]{1,0:T(8,128)(2,1)}) %all-gather.7.cloned.1.call-update) | async-done | bytes 2097168 | tf_op jit(solution)/shard_map/all_gather | solution.py:105
  101.3 2.2 fusion.30
  103.5 0.8 copy-done.3
  104.5 0.7 fusion.44
  105.4 30.6 %all_gather.28 = bf16[32,1024]{0,1:T(8,128)(2,1)S(1)} all-gather(bf16[32,32]{0,1:T(8,128)(2,1)S(1)} %copy.120), channel_id=1, replica_groups=mesh['grp'=16,'tok'=32] {'tok'}, dimensions={1}, use_global_device_ids=true | all-gather | bytes 67584 | tf_op jit(solution)/shard_map/all_gather | solution.py:140
  136.0 0.7 copy.121
  137.7 2.4 broadcast_in_dim.41
  140.2 2.6 broadcast_in_dim.42
  142.7 31.0 %all-gather = bf16[1,512,512]{2,1,0:T(8,128)(2,1)S(1)} all-gather(bf16[1,16,512]{2,1,0:T(8,128)(2,1)S(1)} %copy-done.5), channel_id=2, replica_groups=mesh['grp'=16,'tok'=32] {'tok'}, dimensions={1}, use_global_device_ids=true | all-gather | bytes 540672 | tf_op jit(solution)/shard_map/all_gather | solution.py:129
  174.0 0.9 copy.112
  175.0 9.2 %reduce-window.11 = s32[32,8,128]{2,1,0:T(8,128)S(1)} reduce-window(s32[32,8,128]{2,1,0:T(8,128)S(1)} %fusion.37, s32[]{:T(128)} %constant.34.clone.1), window={size=1x1x128 pad=0_0x0_0x127_0}, to_apply=%region_9.10 | reduce-window | flops 4161536 | bytes 262148 | tf_op jit(solution)/shard_map/reduce-window.1
  185.3 0.7 pad_maximum_fusion
  186.0 1.8 multiply_reduce_fusion
  187.8 3.8 fusion.45
  191.6 2.9 copy.117
  194.6 2.9 copy.115
  197.5 3.5 fusion
  201.0 4.4 fusion.1
  205.4 1.9 copy-done
  207.3 0.5 fusion.13
  207.9 11.2 %fusion.3 = f32[4,256,64]{1,2,0:T(8,128)} fusion(bf16[4,4096,64]{1,2,0:T(8,128)(2,1)} %bitcast.105, f32[4,256,4096]{2,1,0:T(8,128)} %copy-done, f32[4,256]{1,0:T(4,128)S(1)} %get-tuple-element.15, pred[256,4096]{1,0:T(8,128)(4,1)S(1)} %broadcast_in_dim.42), kind=kOutput, calls=%fused_computation.8 | convolution fusion | flops 553648128 | bytes 20189184 | tf_op jit(solution)/shard_map/kqn,knd->kqd/dot_general | solution.py:70
  219.1 1.6 fusion.21
  221.0 16.5 %all-gather.11.cloned.1.call-done = bf16[512,1024]{1,0:T(8,128)(2,1)} async-done(((bf16[32,1024]{1,0:T(8,128)(2,1)}), bf16[512,1024]{1,0:T(8,128)(2,1)}) %all-gather.11.cloned.1.call-update) | async-done | bytes 1048592 | tf_op jit(solution)/shard_map/all_gather | solution.py:144
  237.6 1.6 multiply_reduce_fusion.1
  239.3 14.7 %scatter_custom_fusion = bf16[1280,1024]{1,0:T(8,128)(2,1)} fusion(s32[1024]{0:T(1024)S(1)} %bitcast.118, bf16[128,1024]{1,0:T(8,128)(2,1)S(1)} %multiply_convert_fusion, s32[1024]{0:T(1024)S(1)} %broadcast_clamp_fusion.1, bf16[]{:T(256)} %constant.67.clone.1), kind=kCustom, calls=%fused_computation.19 | custom fusion | bytes 2621442 | tf_op jit(solution)/shard_map/scatter | solution.py:160
  254.1 12.8 %all-to-all-start = ((bf16[32,40,1024]{2,1,0:T(8,128)(2,1)}), bf16[32,40,1024]{2,1,0:T(8,128)(2,1)S(1)}, u32[]{:S(2)}, u32[]{:S(2)}) async-start(bf16[32,40,1024]{2,1,0:T(8,128)(2,1)} %bitcast.31), calls=%async_computation | async-start | bytes 5242880 | tf_op jit(solution)/shard_map/all_to_all | solution.py:162
  266.9 0.5 all-gather.13.cloned.1.call-update
  267.5 0.5 all-gather.15.cloned.1.call-update
  268.0 61.4 %all-gather.13.cloned.1.call-done = bf16[1,1024,1024]{2,1,0:T(8,128)(2,1)} async-done(((bf16[1,64,1024]{2,1,0:T(8,128)(2,1)}), bf16[1,1024,1024]{2,1,0:T(8,128)(2,1)}) %all-gather.13.cloned.1.call-update) | async-done | bytes 2097168 | tf_op jit(solution)/shard_map/all_gather | solution.py:169
  329.4 60.2 %all-to-all-done = bf16[32,40,1024]{2,1,0:T(8,128)(2,1)S(1)} async-done(((bf16[32,40,1024]{2,1,0:T(8,128)(2,1)}), bf16[32,40,1024]{2,1,0:T(8,128)(2,1)S(1)}, u32[]{:S(2)}, u32[]{:S(2)}) %all-to-all-start) | async-done | bytes 2621472 | tf_op jit(solution)/shard_map/all_to_all | solution.py:162
  389.6 6.2 %convolution_bitcast_fusion = f32[1,1280,1024]{2,1,0:T(8,128)} fusion(bf16[1280,1024]{1,0:T(8,128)(2,1)S(1)} %bitcast.104, bf16[1,1024,1024]{2,1,0:T(8,128)(2,1)} %all-gather.13.cloned.1.call-done), kind=kOutput, calls=%fused_computation.10 | convolution fusion | flops 2684354560 | bytes 9961472 | tf_op jit(solution)/shard_map/erd,edf->erf/dot_general | solution.py:166
  395.8 4.4 fusion.7
  400.2 18.2 %copy.137 = bf16[1,1280,1024]{2,0,1:T(2,128)(2,1)} copy(bf16[1,1280,1024]{2,1,0:T(8,128)(2,1)S(1)} %fusion.7) | data formatting | bytes 5242880 | tf_op jit(solution)/shard_map/convert_element_type | solution.py:179
  418.4 0.5 broadcast.297
  418.9 15.6 %reduce = bf16[1280,1024]{1,0:T(8,128)(2,1)S(1)} reduce(bf16[1280,1,1024]{2,1,0:T(2,128)(2,1)} %bitcast.99, bf16[]{:T(256)} %broadcast.297), dimensions={1}, to_apply=%bitcast.97.reduce_sub_computation | reduce | bytes 5242882
  434.4 3.0 reshape.386
  437.4 6.9 %all-to-all-start.1 = ((bf16[32,2,20480]{2,1,0:T(2,128)(2,1)}), bf16[32,2,20480]{2,1,0:T(2,128)(2,1)S(1)}, u32[]{:S(2)}, u32[]{:S(2)}) async-start(bf16[32,2,20480]{2,1,0:T(2,128)(2,1)} %reshape.386), calls=%async_computation.1 | async-start | bytes 5242880 | tf_op jit(solution)/shard_map/all_to_all | solution.py:180
  444.5 122.6 %all-to-all-done.1 = bf16[32,2,20480]{2,1,0:T(2,128)(2,1)S(1)} async-done(((bf16[32,2,20480]{2,1,0:T(2,128)(2,1)}), bf16[32,2,20480]{2,1,0:T(2,128)(2,1)S(1)}, u32[]{:S(2)}, u32[]{:S(2)}) %all-to-all-start.1) | async-done | bytes 2621472 | tf_op jit(solution)/shard_map/all_to_all | solution.py:180
  567.1 7.2 %reshape.387 = bf16[1280,1,1024]{2,1,0:T(2,128)(2,1)} reshape(bf16[32,2,20480]{2,1,0:T(2,128)(2,1)S(1)} %all-to-all-done.1) | data formatting | bytes 5242880
  574.3 3.5 copy.136
  577.8 5.4 gather_fusion
  583.2 2.9 fusion.6
  586.1 0.8 fusion.29
  (78 shorter events, 3.8 us)
Async XLA Ops:
  7.2 94.1 %all-gather.7.cloned.1.call-start = ((), (), s32[]{:S(2)}) async-start(), calls=%async_computation.2 | async-start | bytes 2228224 | tf_op jit(solution)/shard_map/all_gather | solution.py:105
  42.3 63.1 %copy-start.7 = (bf16[32,32]{1,0:T(8,128)(2,1)S(1)}, bf16[32,32]{1,0:T(8,128)(2,1)}, u32[]{:S(2)}) copy-start(bf16[32,32]{1,0:T(8,128)(2,1)} %param.18) | copy-start | bytes 6148
  43.1 144.7 %all-gather.9.cloned.1.call-start = ((), (), s32[]{:S(2)}) async-start(), calls=%async_computation.3 | async-start | bytes 4325376 | tf_op jit(solution)/shard_map/all_gather | solution.py:131
  46.1 90.9 %copy-start.6 = (s32[1,128,8]{1,2,0:T(8,128)S(1)}, s32[1,128,8]{1,2,0:T(8,128)}, u32[]{:S(2)}) copy-start(s32[1,128,8]{1,2,0:T(8,128)} %param.14) | copy-start | bytes 12292
  103.5 0.8 copy-start.3
  105.3 132.3 %all-gather.11.cloned.1.call-start = ((), (), s32[]{:S(2)}) async-start(), calls=%async_computation.4 | async-start | bytes 1114112 | tf_op jit(solution)/shard_map/all_gather | solution.py:144
  137.7 5.0 copy-start.5
  142.7 42.0 %slice-start = ((f32[128,1024]{1,0:T(8,128)}), f32[128,512]{1,0:T(8,128)S(1)}, s32[]{:S(2)}) async-start(f32[128,1024]{1,0:T(8,128)} %copy-done.3), calls=%async_computation.7 | async-start | bytes 524288 | tf_op jit(solution)/shard_map/slice | solution.py:108
  201.0 6.3 %copy-start = (f32[4,256,4096]{2,1,0:T(8,128)}, f32[4,256,4096]{2,1,0:T(8,128)S(1)}, u32[]{:S(2)}) copy-start(f32[4,256,4096]{2,1,0:T(8,128)S(1)} %get-tuple-element.22) | copy-start | bytes 50331652
  201.0 6.3 %copy-start.1 = (f32[4,256,512]{2,1,0:T(8,128)S(1)}, f32[4,256,512]{2,1,0:T(8,128)}, u32[]{:S(2)}) copy-start(f32[4,256,512]{2,1,0:T(8,128)} %get-tuple-element.20) | copy-start | bytes 6291460
  207.9 11.2 %copy-start.4 = (bf16[512,256]{0,1:T(8,128)(2,1)S(1)}, bf16[512,256]{0,1:T(8,128)(2,1)}, u32[]{:S(2)}) copy-start(bf16[512,256]{0,1:T(8,128)(2,1)} %copy.112) | copy-start | bytes 786436
  219.1 18.4 %copy-start.2 = (bf16[1,128,1024]{2,1,0:T(8,128)(2,1)S(1)}, bf16[1,128,1024]{2,1,0:T(8,128)(2,1)}, u32[]{:S(2)}) copy-start(bf16[1,128,1024]{2,1,0:T(8,128)(2,1)} %param.11) | copy-start | bytes 786436
  219.1 20.1 %copy-start.8 = (f32[1024]{0:T(1024)S(1)}, f32[1024]{0:T(1024)}, u32[]{:S(2)}) copy-start(f32[1024]{0:T(1024)} %param.19) | copy-start | bytes 12292
  254.1 135.6 %all-to-all-start = ((bf16[32,40,1024]{2,1,0:T(8,128)(2,1)}), bf16[32,40,1024]{2,1,0:T(8,128)(2,1)S(1)}, u32[]{:S(2)}, u32[]{:S(2)}) async-start(bf16[32,40,1024]{2,1,0:T(8,128)(2,1)} %bitcast.31), calls=%async_computation | async-start | bytes 5242880 | tf_op jit(solution)/shard_map/all_to_all | solution.py:162
  266.9 62.5 %all-gather.13.cloned.1.call-start = ((), (), s32[]{:S(2)}) async-start(), calls=%async_computation.5 | async-start | bytes 2228224 | tf_op jit(solution)/shard_map/all_gather | solution.py:169
  267.5 128.3 %all-gather.15.cloned.1.call-start = ((), (), s32[]{:S(2)}) async-start(), calls=%async_computation.6 | async-start | bytes 1114112 | tf_op jit(solution)/shard_map/all_gather | solution.py:177
  437.4 6.9 %copy-start.9 = (f32[1,128,8]{1,2,0:T(8,128)S(1)}, f32[1,128,8]{1,2,0:T(8,128)}, u32[]{:S(2)}) copy-start(f32[1,128,8]{1,2,0:T(8,128)} %param.15) | copy-start | bytes 12292
  437.4 129.7 %all-to-all-start.1 = ((bf16[32,2,20480]{2,1,0:T(2,128)(2,1)}), bf16[32,2,20480]{2,1,0:T(2,128)(2,1)S(1)}, u32[]{:S(2)}, u32[]{:S(2)}) async-start(bf16[32,2,20480]{2,1,0:T(2,128)(2,1)} %reshape.386), calls=%async_computation.1 | async-start | bytes 5242880 | tf_op jit(solution)/shard_map/all_to_all | solution.py:180
Sparse Core Ops, SparseCore 0:
  43.2 58.0 all-gather.6
  105.4 73.6 all-gather.8
  182.1 55.3 all-gather.10
  270.4 58.9 all-gather.12
  332.3 57.4 all-gather.14
where the time goes:
time: 594 us; the launch traced here: 593 us
  waiting for transfers between devices  317 us (53%)
  blocking collectives  96.7 us (16%)
  local copies, waits for them, and re-layouts  74.3 us (13%)
  other arithmetic  38.8 us (7%)
  matrix products  32.4 us (5%)
  starting transfers between devices  19.9 us (3%)
  between operations  14.2 us (2%)
    all_to_all x1, waiting for transfers between devices, local(): lax.all_to_all(expert_result, 'tok', split_axis=1, concat_axis=0, tiled=T...  123 us
    all_gather x1, waiting for transfers between devices, local(): lax.all_gather(expert_gate_up, 'grp', axis=1, tiled=True)  61.4 us
    all_to_all x1, waiting for transfers between devices, local(): lax.all_to_all(outgoing.reshape(EXPERTS, CAP, model_width), 'tok', split_...  60.2 us
    all_gather x1, waiting for transfers between devices, local(): lax.all_gather(columns, 'grp', axis=0, tiled=True)  55.2 us
    all_gather x1, blocking collectives, local(): columns = lax.all_gather(w_qkv, 'tok', axis=1, tiled=True)  35 us
    all_gather x1, blocking collectives, local(): lax.all_gather(prefix_cache[0], 'tok', axis=0, tiled=True)  31 us
    all_gather x1, blocking collectives, local(): out_columns = lax.all_gather(w_out, 'tok', axis=1, tiled=True)  30.6 us
    convert_element_type x1, local copies, waits for them, and re-layouts, local(): expert_result = jnp.einsum('erf,efd->erd', sliced, lax.all_gather(expert_...  18.2 us
  transfers between devices with their start and end apart: 7, of which 5 were waited for; matrix products, arithmetic and copies ran while one was open for 10% of the time, Pallas kernels for 0%

commit v1 on v0

--- a/solution.py
+++ b/solution.py
@@ -177,8 +177,11 @@
         lax.all_gather(expert_down, "grp", axis=1, tiled=True),
         preferred_element_type=jnp.float32,
     ).astype(jnp.bfloat16)
-    returned = lax.all_to_all(
-        expert_result, "tok", split_axis=1, concat_axis=0, tiled=True
+    returned = jnp.concatenate(
+        lax.all_to_all(
+            jnp.stack(jnp.split(expert_result, lax.axis_size("tok"), axis=1)), "tok", 0, 0
+        ),
+        axis=0,
     ).reshape(EXPERTS * CAP, -1)
     weighted = returned[slot_index].astype(jnp.float32) * gates[0].reshape(-1)[:, None]
     moe_out = jnp.sum(weighted.reshape(tok_count, TOP, -1), axis=1)

time: 594 us -> 566 us (0.953)
  other arithmetic: 38.8 us -> 23.3 us
  local copies, waits for them, and re-layouts: 74.3 us -> 62.2 us
    convert_element_type x1 -> x0, local copies, waits for them, and re-layouts: 18.2 us -> none  [local(): expert_result = jnp.einsum('erf,efd->erd', sliced, lax.all_gather(expert_...]
    unnamed x1 -> x0, other arithmetic: 15.6 us -> none
    unnamed x26 -> x53, local copies, waits for them, and re-layouts: 17.1 us -> 22.5 us
  transfers between devices with their start and end apart: 7 -> 7, of which waited for: 5 -> 5; matrix products, arithmetic and copies ran while one was open for 10% -> 11% of each run, Pallas kernels for 0% -> 0%
where the time goes in v1:
time: 566 us
  waiting for transfers between devices  317 us (56%)
  blocking collectives  96.7 us (17%)
  local copies, waits for them, and re-layouts  62.2 us (11%)
  matrix products  32.4 us (6%)
  other arithmetic  23.3 us (4%)
  starting transfers between devices  19.9 us (4%)
  between operations  14.2 us (3%)
    all_to_all x1, waiting for transfers between devices, local(): lax.all_to_all(jnp.stack(jnp.split(expert_result, lax.axis_size('tok'), a...  123 us
    all_gather x1, waiting for transfers between devices, local(): lax.all_gather(expert_gate_up, 'grp', axis=1, tiled=True)  61.4 us
    all_to_all x1, waiting for transfers between devices, local(): lax.all_to_all(outgoing.reshape(EXPERTS, CAP, model_width), 'tok', split_...  60.2 us
    all_gather x1, waiting for transfers between devices, local(): lax.all_gather(columns, 'grp', axis=0, tiled=True)  55.2 us
    all_gather x1, blocking collectives, local(): columns = lax.all_gather(w_qkv, 'tok', axis=1, tiled=True)  35 us
    all_gather x1, blocking collectives, local(): lax.all_gather(prefix_cache[0], 'tok', axis=0, tiled=True)  31 us
    all_gather x1, blocking collectives, local(): out_columns = lax.all_gather(w_out, 'tok', axis=1, tiled=True)  30.6 us
    unnamed x53, local copies, waits for them, and re-layouts  22.5 us
  transfers between devices with their start and end apart: 7, of which 5 were waited for; matrix products, arithmetic and copies ran while one was open for 11% of the time, Pallas kernels for 0%

profile of v1, /device:TPU:32, one launch (start us, length us, event | category | flops | bytes accessed | tf_op | source)
XLA Modules:
  0.0 565.7 jit_solution(14187997027213166854)
XLA Ops:
  7.2 35.0 %all_gather.24 = bf16[64,1024]{0,1:T(8,128)(2,1)S(1)} all-gather(bf16[64,32]{0,1:T(8,128)(2,1)} %param.17), channel_id=1, replica_groups=mesh['grp'=16,'tok'=32] {'tok'}, dimensions={1}, use_global_device_ids=true | all-gather | bytes 135168 | tf_op jit(solution)/shard_map/all_gather | solution.py:101
  42.3 0.8 copy.82
  43.1 0.8 reduce-window.10
  44.1 0.7 fusion.70
  44.8 1.1 fusion.26
  46.1 55.2 %all-gather.7.cloned.1.call-done = bf16[1024,1024]{1,0:T(8,128)(2,1)} async-done(((bf16[64,1024]{1,0:T(8,128)(2,1)}), bf16[1024,1024]{1,0:T(8,128)(2,1)}) %all-gather.7.cloned.1.call-update) | async-done | bytes 2097168 | tf_op jit(solution)/shard_map/all_gather | solution.py:105
  101.3 2.2 fusion.30
  103.5 0.8 copy-done.3
  104.5 0.7 fusion.76
  105.4 30.6 %all_gather.28 = bf16[32,1024]{0,1:T(8,128)(2,1)S(1)} all-gather(bf16[32,32]{0,1:T(8,128)(2,1)S(1)} %copy.96), channel_id=1, replica_groups=mesh['grp'=16,'tok'=32] {'tok'}, dimensions={1}, use_global_device_ids=true | all-gather | bytes 67584 | tf_op jit(solution)/shard_map/all_gather | solution.py:140
  136.0 0.7 copy.97
  137.7 2.4 broadcast_in_dim.41
  140.2 2.6 broadcast_in_dim.42
  142.7 31.0 %all-gather = bf16[1,512,512]{2,1,0:T(8,128)(2,1)S(1)} all-gather(bf16[1,16,512]{2,1,0:T(8,128)(2,1)S(1)} %copy-done.5), channel_id=2, replica_groups=mesh['grp'=16,'tok'=32] {'tok'}, dimensions={1}, use_global_device_ids=true | all-gather | bytes 540672 | tf_op jit(solution)/shard_map/all_gather | solution.py:129
  174.0 0.9 copy.88
  175.0 9.2 %reduce-window.11 = s32[32,8,128]{2,1,0:T(8,128)S(1)} reduce-window(s32[32,8,128]{2,1,0:T(8,128)S(1)} %fusion.37, s32[]{:T(128)} %constant.34.clone.1), window={size=1x1x128 pad=0_0x0_0x127_0}, to_apply=%region_9.10 | reduce-window | flops 4161536 | bytes 262148 | tf_op jit(solution)/shard_map/reduce-window.1
  185.3 0.7 pad_maximum_fusion
  186.0 1.8 multiply_reduce_fusion
  187.8 3.8 fusion.77
  191.6 2.9 copy.93
  194.6 2.9 copy.91
  197.5 3.5 fusion
  201.0 4.4 fusion.1
  205.4 1.9 copy-done
  207.9 11.2 %fusion.3 = f32[4,256,64]{1,2,0:T(8,128)} fusion(bf16[4,4096,64]{1,2,0:T(8,128)(2,1)} %bitcast.225, f32[4,256,4096]{2,1,0:T(8,128)} %copy-done, f32[4,256]{1,0:T(4,128)S(1)} %get-tuple-element.15, pred[256,4096]{1,0:T(8,128)(4,1)S(1)} %broadcast_in_dim.42), kind=kOutput, calls=%fused_computation.8 | convolution fusion | flops 553648128 | bytes 20189184 | tf_op jit(solution)/shard_map/kqn,knd->kqd/dot_general | solution.py:70
  219.1 1.6 fusion.21
  221.0 16.5 %all-gather.11.cloned.1.call-done = bf16[512,1024]{1,0:T(8,128)(2,1)} async-done(((bf16[32,1024]{1,0:T(8,128)(2,1)}), bf16[512,1024]{1,0:T(8,128)(2,1)}) %all-gather.11.cloned.1.call-update) | async-done | bytes 1048592 | tf_op jit(solution)/shard_map/all_gather | solution.py:144
  237.6 1.6 multiply_reduce_fusion.1
  239.3 14.7 %scatter_custom_fusion = bf16[1280,1024]{1,0:T(8,128)(2,1)} fusion(s32[1024]{0:T(1024)S(1)} %bitcast.238, bf16[128,1024]{1,0:T(8,128)(2,1)S(1)} %multiply_convert_fusion, s32[1024]{0:T(1024)S(1)} %broadcast_clamp_fusion.1, bf16[]{:T(256)} %constant.67.clone.1), kind=kCustom, calls=%fused_computation.18 | custom fusion | bytes 2621442 | tf_op jit(solution)/shard_map/scatter | solution.py:160
  254.1 12.8 %all-to-all-start = ((bf16[32,40,1024]{2,1,0:T(8,128)(2,1)}), bf16[32,40,1024]{2,1,0:T(8,128)(2,1)S(1)}, u32[]{:S(2)}, u32[]{:S(2)}) async-start(bf16[32,40,1024]{2,1,0:T(8,128)(2,1)} %bitcast.31), calls=%async_computation | async-start | bytes 5242880 | tf_op jit(solution)/shard_map/all_to_all | solution.py:162
  268.0 61.4 %all-gather.13.cloned.1.call-done = bf16[1,1024,1024]{2,1,0:T(8,128)(2,1)} async-done(((bf16[1,64,1024]{2,1,0:T(8,128)(2,1)}), bf16[1,1024,1024]{2,1,0:T(8,128)(2,1)}) %all-gather.13.cloned.1.call-update) | async-done | bytes 2097168 | tf_op jit(solution)/shard_map/all_gather | solution.py:169
  329.4 60.2 %all-to-all-done = bf16[32,40,1024]{2,1,0:T(8,128)(2,1)S(1)} async-done(((bf16[32,40,1024]{2,1,0:T(8,128)(2,1)}), bf16[32,40,1024]{2,1,0:T(8,128)(2,1)S(1)}, u32[]{:S(2)}, u32[]{:S(2)}) %all-to-all-start) | async-done | bytes 2621472 | tf_op jit(solution)/shard_map/all_to_all | solution.py:162
  389.6 6.2 %convolution_bitcast_fusion = f32[1,1280,1024]{2,1,0:T(8,128)} fusion(bf16[1280,1024]{1,0:T(8,128)(2,1)S(1)} %bitcast.224, bf16[1,1024,1024]{2,1,0:T(8,128)(2,1)} %all-gather.13.cloned.1.call-done), kind=kOutput, calls=%fused_computation.10 | convolution fusion | flops 2684354560 | bytes 9961472 | tf_op jit(solution)/shard_map/erd,edf->erf/dot_general | solution.py:166
  395.8 4.4 fusion.7
  406.5 0.6 fusion.59
  407.7 0.6 fusion.57
  408.4 0.6 fusion.56
  409.7 0.6 fusion.54
  411.6 0.6 fusion.51
  414.1 0.6 fusion.47
  416.6 0.6 fusion.43
  417.9 0.6 fusion.41
  419.8 0.6 fusion.38
  420.5 6.9 %all-to-all-start.1 = ((bf16[32,1,40,1024]{3,2,1,0:T(8,128)(2,1)}), bf16[32,1,40,1024]{3,2,1,0:T(8,128)(2,1)S(1)}, u32[]{:S(2)}, u32[]{:S(2)}) async-start(bf16[32,1,40,1024]{3,2,1,0:T(8,128)(2,1)} %fusion.38), calls=%async_computation.1 | async-start | bytes 5242880 | tf_op jit(solution)/shard_map/all_to_all | solution.py:181
  427.5 122.6 %all-to-all-done.1 = bf16[32,1,40,1024]{3,2,1,0:T(8,128)(2,1)S(1)} async-done(((bf16[32,1,40,1024]{3,2,1,0:T(8,128)(2,1)}), bf16[32,1,40,1024]{3,2,1,0:T(8,128)(2,1)S(1)}, u32[]{:S(2)}, u32[]{:S(2)}) %all-to-all-start.1) | async-done | bytes 2621472 | tf_op jit(solution)/shard_map/all_to_all | solution.py:181
  550.1 5.4 gather_fusion
  555.5 2.9 fusion.6
  558.4 0.8 fusion.29
  (104 shorter events, 19.9 us)
Async XLA Ops:
  7.2 94.1 %all-gather.7.cloned.1.call-start = ((), (), s32[]{:S(2)}) async-start(), calls=%async_computation.2 | async-start | bytes 2228224 | tf_op jit(solution)/shard_map/all_gather | solution.py:105
  42.3 63.1 %copy-start.7 = (bf16[32,32]{1,0:T(8,128)(2,1)S(1)}, bf16[32,32]{1,0:T(8,128)(2,1)}, u32[]{:S(2)}) copy-start(bf16[32,32]{1,0:T(8,128)(2,1)} %param.18) | copy-start | bytes 6148
  43.1 144.7 %all-gather.9.cloned.1.call-start = ((), (), s32[]{:S(2)}) async-start(), calls=%async_computation.3 | async-start | bytes 4325376 | tf_op jit(solution)/shard_map/all_gather | solution.py:131
  46.1 90.9 %copy-start.6 = (s32[1,128,8]{1,2,0:T(8,128)S(1)}, s32[1,128,8]{1,2,0:T(8,128)}, u32[]{:S(2)}) copy-start(s32[1,128,8]{1,2,0:T(8,128)} %param.14) | copy-start | bytes 12292
  103.5 0.8 copy-start.3
  105.3 132.3 %all-gather.11.cloned.1.call-start = ((), (), s32[]{:S(2)}) async-start(), calls=%async_computation.4 | async-start | bytes 1114112 | tf_op jit(solution)/shard_map/all_gather | solution.py:144
  137.7 5.0 copy-start.5
  142.7 42.0 %slice-start = ((f32[128,1024]{1,0:T(8,128)}), f32[128,512]{1,0:T(8,128)S(1)}, s32[]{:S(2)}) async-start(f32[128,1024]{1,0:T(8,128)} %copy-done.3), calls=%async_computation.7 | async-start | bytes 524288 | tf_op jit(solution)/shard_map/slice | solution.py:108
  201.0 6.3 %copy-start = (f32[4,256,4096]{2,1,0:T(8,128)}, f32[4,256,4096]{2,1,0:T(8,128)S(1)}, u32[]{:S(2)}) copy-start(f32[4,256,4096]{2,1,0:T(8,128)S(1)} %get-tuple-element.22) | copy-start | bytes 50331652
  201.0 6.3 %copy-start.1 = (f32[4,256,512]{2,1,0:T(8,128)S(1)}, f32[4,256,512]{2,1,0:T(8,128)}, u32[]{:S(2)}) copy-start(f32[4,256,512]{2,1,0:T(8,128)} %get-tuple-element.20) | copy-start | bytes 6291460
  207.9 11.2 %copy-start.4 = (bf16[512,256]{0,1:T(8,128)(2,1)S(1)}, bf16[512,256]{0,1:T(8,128)(2,1)}, u32[]{:S(2)}) copy-start(bf16[512,256]{0,1:T(8,128)(2,1)} %copy.88) | copy-start | bytes 786436
  219.1 18.4 %copy-start.2 = (bf16[1,128,1024]{2,1,0:T(8,128)(2,1)S(1)}, bf16[1,128,1024]{2,1,0:T(8,128)(2,1)}, u32[]{:S(2)}) copy-start(bf16[1,128,1024]{2,1,0:T(8,128)(2,1)} %param.11) | copy-start | bytes 786436
  219.1 20.1 %copy-start.8 = (f32[1024]{0:T(1024)S(1)}, f32[1024]{0:T(1024)}, u32[]{:S(2)}) copy-start(f32[1024]{0:T(1024)} %param.19) | copy-start | bytes 12292
  254.1 135.6 %all-to-all-start = ((bf16[32,40,1024]{2,1,0:T(8,128)(2,1)}), bf16[32,40,1024]{2,1,0:T(8,128)(2,1)S(1)}, u32[]{:S(2)}, u32[]{:S(2)}) async-start(bf16[32,40,1024]{2,1,0:T(8,128)(2,1)} %bitcast.31), calls=%async_computation | async-start | bytes 5242880 | tf_op jit(solution)/shard_map/all_to_all | solution.py:162
  266.9 62.5 %all-gather.13.cloned.1.call-start = ((), (), s32[]{:S(2)}) async-start(), calls=%async_computation.5 | async-start | bytes 2228224 | tf_op jit(solution)/shard_map/all_gather | solution.py:169
  267.5 128.3 %all-gather.15.cloned.1.call-start = ((), (), s32[]{:S(2)}) async-start(), calls=%async_computation.6 | async-start | bytes 1114112 | tf_op jit(solution)/shard_map/all_gather | solution.py:177
  420.5 6.9 %copy-start.9 = (f32[1,128,8]{1,2,0:T(8,128)S(1)}, f32[1,128,8]{1,2,0:T(8,128)}, u32[]{:S(2)}) copy-start(f32[1,128,8]{1,2,0:T(8,128)} %param.15) | copy-start | bytes 12292
  420.5 129.7 %all-to-all-start.1 = ((bf16[32,1,40,1024]{3,2,1,0:T(8,128)(2,1)}), bf16[32,1,40,1024]{3,2,1,0:T(8,128)(2,1)S(1)}, u32[]{:S(2)}, u32[]{:S(2)}) async-start(bf16[32,1,40,1024]{3,2,1,0:T(8,128)(2,1)} %fusion.38), calls=%async_computation.1 | async-start | bytes 5242880 | tf_op jit(solution)/shard_map/all_to_all | solution.py:181
Sparse Core Ops, SparseCore 0:
  43.2 58.0 all-gather.6
  105.4 73.6 all-gather.8
  182.1 55.3 all-gather.10
  270.4 58.9 all-gather.12
  332.3 57.4 all-gather.14
